TPU v7x, 32 devices: a whole 2x2x4 slice. The times are simulated.
32 devices in a mesh: groups: 1, row: 8 (over z, y), col: 2 (over x), chan: 2 (over core).
Axes of the slice: x: 2, y: 2, z: 4, core: 2. Of those that a mesh axis runs over, the one named last changes fastest.
Arguments:
- pair: bfloat16 [256, 128, 256], P(('groups', 'row'), None, 'col'), may hold values from -6 to 6
- grad_x: bfloat16 [256, 128, 256], P(('groups', 'row'), 'chan', 'col'), may hold values from -0.375 to 0.375
- ln_gain: float32 [128], replicated, may hold values from 0.5 to 1.5
- ln_bias: float32 [128], replicated, may hold values from -3 to 3
- weights: bfloat16 [4, 128, 128], P(None, None, 'chan'), may hold values from -0.5 to 0.5
- chain_id: int32 [256], P('groups'), may hold values from 0 to 15, never falling along the last dimension, each value on 1 to 32 neighbouring positions
- kept: int32 [16, 16], P('groups'), may hold values 0 or 1
Outputs:
- grad_pair: float32 [256, 128, 256], P(('groups', 'row'), 'chan', 'col')
Inputs may be any that keep to these rules, and one draw needn't show every extreme that they name: `chain_id`: chain numbers never fall along the residues; each chain holds 1 to 32 residues.
All inputs are finite; a program needn't handle non-finite values.
Results may differ from a plain program's by a relative error of at most 0.0055.
Values may be sent and summed in bfloat16 or wider, within the bound.
A program may use at most 128 MiB of HBM per device.

v0:
```python
import functools

import jax
import jax.numpy as jnp
from jax import lax
from jax.experimental import pallas as pl
from jax.experimental.pallas import tpu as pltpu
from jax.sharding import PartitionSpec as P

MESH = pl.DeviceIdType.MESH
F32 = jnp.float32
BF16 = jnp.bfloat16
CHUNKS = 4


def normalized(pair_ref, i):
    values = pair_ref[i].astype(F32)
    mean = jnp.mean(values, axis=0, keepdims=True)
    centered = values - mean
    inverse = lax.rsqrt(jnp.mean(centered * centered, axis=0, keepdims=True) + 1e-05)
    return mean, centered, inverse


def main_kernel(
    dims,
    pair_ref,
    grad_ref,
    gain_ref,
    bias_ref,
    proj_ref,
    chain_ref,
    kept_ref,
    out_ref,
    full,
    left,
    right,
    grad_in,
    grad_wide,
    packed,
    packed_all,
    mask_ref,
    grad_left,
    grad_right,
    stat_buf,
    scaled_in,
    stat_in,
    fwd_send,
    fwd_recv,
    bwd_send,
    bwd_recv,
    pass_send,
    pass_recv,
    x_send,
    x_recv,
    a_send,
    a_recv,
    swap_send,
    swap_recv,
    end_send,
    end_recv,
):
    R, X, A = dims
    rows, width, cols = pair_ref.shape
    hidden = grad_ref.shape[1]
    pack = cols // rows
    groups = packed.shape[1]
    total = R * rows
    pitch = left.shape[0] // hidden
    gpitch = grad_wide.shape[1] // rows
    half = rows // A
    step_rows = half // CHUNKS
    T = R // 2
    last = T - 1
    share = width // A

    g = lax.axis_index("groups")
    r = lax.axis_index("row")
    x = lax.axis_index("col")
    a = lax.axis_index("chan")
    sib = 1 - a

    def row_of(p):
        p = (p + R) % R
        return jnp.where(p < T, 2 * p, 2 * (R - 1 - p) + 1)

    p = jnp.where(r % 2 == 0, r // 2, R - 1 - r // 2)
    nxt = row_of(p + 1)
    prv = row_of(p - 1)

    barrier = pltpu.get_barrier_semaphore()
    peers = [(g, r, x, sib)]
    peers += [(g, r, (x + d) % X, a) for d in range(1, X)]
    peers += [(g, (r + d) % R, x, a) for d in range(1, R)]
    for peer in peers:
        pl.semaphore_signal(barrier, inc=1, device_id=peer, device_id_type=MESH)

    gain = jnp.broadcast_to(gain_ref[...], (cols, width)).T
    bias = jnp.broadcast_to(bias_ref[...], (cols, width)).T

    def normalize(core, l, carry):
        i = core * half + l
        mean, centered, inverse = normalized(pair_ref, i)
        full[r, i] = ((centered * inverse) * gain + bias).astype(BF16)
        return carry

    lax.fori_loop(0, half, functools.partial(normalize, a), 0, unroll=4)
    pl.semaphore_wait(barrier, len(peers))

    def ring(t, c, forward):
        block = row_of(p - t) if forward else row_of(p + t)
        at = full.at[block, pl.ds(a * half + c * step_rows, step_rows)]
        return pltpu.make_async_remote_copy(
            src_ref=at,
            dst_ref=at,
            send_sem=(fwd_send if forward else bwd_send).at[t, c],
            recv_sem=(fwd_recv if forward else bwd_recv).at[t, c],
            device_id=(g, nxt if forward else prv, x, a),
            device_id_type=MESH,
        )

    def got(t, c, forward):
        block = row_of(p - 1 - t) if forward else row_of(p + 1 + t)
        at = full.at[block, pl.ds(a * half + c * step_rows, step_rows)]
        return pltpu.make_async_copy(at, at, (fwd_recv if forward else bwd_recv).at[t, c])

    def passed(t, c, forward, core):
        block = row_of(p - 1 - t) if forward else row_of(p + 1 + t)
        at = full.at[block, pl.ds(core * half + c * step_rows, step_rows)]
        side = 0 if forward else 1
        return pltpu.make_async_remote_copy(
            src_ref=at,
            dst_ref=at,
            send_sem=pass_send.at[side, t, c],
            recv_sem=pass_recv.at[side, t, c],
            device_id=(g, r, x, sib),
            device_id_type=MESH,
        )

    def beside(d):
        return pltpu.make_async_remote_copy(
            src_ref=grad_ref,
            dst_ref=grad_in.at[d - 1],
            send_sem=x_send.at[d - 1],
            recv_sem=x_recv.at[d - 1],
            device_id=(g, r, (x + d) % X, a),
            device_id_type=MESH,
        )

    for c in range(CHUNKS):
        if T > 1 or c < CHUNKS // 2:
            ring(0, c, True).start()
        if T > 1 or c >= CHUNKS // 2:
            ring(0, c, False).start()
    for d in range(1, X):
        beside(d).start()

    lax.fori_loop(0, half, functools.partial(normalize, sib), 0, unroll=4)

    chains = kept_ref.shape[0]
    number = lax.broadcasted_iota(jnp.int32, (chains, total), 0)
    row_hot = (number == chain_ref[...]).astype(F32).astype(BF16)
    mine = chain_ref[:, pl.ds(pl.multiple_of(x * cols, cols), cols)]
    number = lax.broadcasted_iota(jnp.int32, (chains, cols), 0)
    col_hot = (number == mine).astype(F32).astype(BF16)
    reach = jnp.dot(kept_ref[...].astype(F32).astype(BF16), col_hot, preferred_element_type=F32)
    mask_ref[...] = lax.dot_general(
        row_hot, reach.astype(BF16), (((0,), (0,)), ((), ())), preferred_element_type=F32
    )

    projection = proj_ref[...]

    def sides(block, l):
        at = block * rows + l
        out = jnp.dot(projection, full[block, l], preferred_element_type=F32)
        mask = mask_ref[pl.ds(at, 1), :]
        lv = mask * jax.nn.sigmoid(out[hidden : 2 * hidden]) * out[:hidden]
        rv = mask * jax.nn.sigmoid(out[3 * hidden :]) * out[2 * hidden : 3 * hidden]
        left[pl.ds(at, hidden, stride=pitch), :] = lv
        right[pl.ds(at, hidden, stride=pitch), :] = rv

    def own_rows(i, carry):
        sides(r, i)
        return carry

    lax.fori_loop(0, rows, own_rows, 0, unroll=4)

    def widen_own(i, carry):
        at = pl.ds(pl.multiple_of(i * gpitch, 8), hidden)
        grad_wide[x, at, :] = grad_ref[i].astype(F32)
        return carry

    lax.fori_loop(0, rows, widen_own, 0)

    def bwd_chunk(t, c):
        return jnp.where(t < last, c, c + CHUNKS // 2)

    def unit(u):
        t = u // CHUNKS
        c = u % CHUNKS
        cb = bwd_chunk(t, c)
        passed(t, c, True, sib).wait_recv()
        passed(t, cb, False, sib).wait_recv()
        fblock = row_of(p - 1 - t)
        bblock = row_of(p + 1 + t)

        def body(l, carry):
            for core in range(A):
                sides(fblock, core * half + c * step_rows + l)
                sides(bblock, core * half + cb * step_rows + l)
            return carry

        lax.fori_loop(0, step_rows, body, 0, unroll=2)

    units = last * CHUNKS + CHUNKS // 2

    def more(t, c, forward):
        split = c < CHUNKS // 2 if forward else c >= CHUNKS // 2
        return jnp.logical_or(t + 1 < last, jnp.logical_and(t + 1 == last, split))

    def ring_step(u, carry):
        t = u // CHUNKS
        c = u % CHUNKS
        cb = bwd_chunk(t, c)
        got(t, c, True).wait()

        @pl.when(more(t, c, True))
        def _():
            ring(t + 1, c, True).start()

        passed(t, c, True, a).start()
        got(t, cb, False).wait()

        @pl.when(more(t, cb, False))
        def _():
            ring(t + 1, cb, False).start()

        passed(t, cb, False, a).start()

        @pl.when(u > 0)
        def _():
            unit(u - 1)

        return carry

    def piece(d):
        to = (r + d) % R
        return pltpu.make_async_remote_copy(
            src_ref=packed.at[to],
            dst_ref=packed_all.at[x, r],
            send_sem=a_send.at[d],
            recv_sem=a_recv.at[d],
            device_id=(g, to, x, a),
            device_id_type=MESH,
        )

    def swap(d, s, col):
        at = packed_all.at[col, s]
        return pltpu.make_async_remote_copy(
            src_ref=at,
            dst_ref=at,
            send_sem=swap_send.at[d, s],
            recv_sem=swap_recv.at[d, s],
            device_id=(g, r, (x + d) % X, a),
            device_id_type=MESH,
        )

    first = min(CHUNKS, units)
    lax.fori_loop(0, first, ring_step, 0)

    for d in range(1, X):
        source = (x + X - d) % X
        beside(d).wait_recv()

        def widen(i, carry):
            at = pl.ds(pl.multiple_of(i * gpitch, 8), hidden)
            grad_wide[source, at, :] = grad_in[d - 1, i].astype(F32)
            return carry

        lax.fori_loop(0, rows, widen, 0)

    def pack_group(k, carry):
        for e in range(X):
            slabs = [
                grad_wide[e, pl.ds((x * groups + k) * pack + m, rows, stride=gpitch), :]
                for m in range(pack)
            ]
            for q in range(pack):
                tile = jnp.concatenate([slab[:, q * rows : (q + 1) * rows] for slab in slabs], axis=1)
                packed[e * pack + q, k] = tile.astype(BF16)
        return carry

    lax.fori_loop(0, groups, pack_group, 0)
    for d in range(1, R):
        piece(d).start()
    packed_all[x, r] = packed[r]

    third = first + (units - first) * 2 // 5
    lax.fori_loop(first, third, ring_step, 0)
    for d in range(1, X):
        swap(d, r, x).start()
    for d0 in range(1, R):
        s = (r + R - d0) % R
        at = packed_all.at[x, s]
        pltpu.make_async_copy(at, at, a_recv.at[d0]).wait()
        for d in range(1, X):
            swap(d, s, x).start()

    lax.fori_loop(third, units, ring_step, 0)
    unit(units - 1)

    for d in range(1, X):
        for s in range(R):
            swap(d, s, (x + X - d) % X).wait_recv()

    def group(k, carry):
        e = k // groups
        k2 = k % groups
        stacked = jnp.concatenate([packed_all[e, s, k2] for s in range(R)], axis=0)
        turned = stacked.T
        for m in range(pack):
            h = k * pack + m
            rh = right[pl.ds(pl.multiple_of(h * pitch, 8), total), :].astype(BF16)
            lh = left[pl.ds(pl.multiple_of(h * pitch, 8), total), :].astype(BF16)
            gx = jnp.concatenate(
                [grad_wide[e2, pl.ds(h, rows, stride=gpitch), :] for e2 in range(X)], axis=1
            ).astype(BF16)
            at = pl.ds(pl.multiple_of(h * rows, 8), rows)
            grad_left[at, :] = jnp.dot(gx, rh, preferred_element_type=F32)
            grad_right[at, :] = jnp.dot(
                turned[m * rows : (m + 1) * rows], lh, preferred_element_type=F32
            )
        return carry

    lax.fori_loop(0, groups * X, group, 0, unroll=4)

    back = projection.astype(F32).T.astype(BF16)
    n = rows // 4

    def send_end(b):
        at = pl.ds(b * n, n)
        return (
            pltpu.make_async_remote_copy(
                src_ref=left.at[pl.ds(pl.multiple_of((sib * rows + b * n) * share, 8), n * share)],
                dst_ref=scaled_in.at[pl.ds(b * n * share, n * share)],
                send_sem=end_send.at[0, b],
                recv_sem=end_recv.at[0, b],
                device_id=(g, r, x, sib),
                device_id_type=MESH,
            ),
            pltpu.make_async_remote_copy(
                src_ref=stat_buf.at[at],
                dst_ref=stat_in.at[at],
                send_sem=end_send.at[1, b],
                recv_sem=end_recv.at[1, b],
                device_id=(g, r, x, sib),
                device_id_type=MESH,
            ),
        )

    def finish_row(i, carry):
        out = jnp.dot(projection, full[r, i], preferred_element_type=F32)
        mask = mask_ref[pl.ds(r * rows + i, 1), :]
        gl = grad_left[pl.ds(i, hidden, stride=rows), :] * mask
        gr = grad_right[pl.ds(i, hidden, stride=rows), :] * mask
        s0 = jax.nn.sigmoid(out[hidden : 2 * hidden])
        s1 = jax.nn.sigmoid(out[3 * hidden :])
        gl = gl * s0
        gr = gr * s1
        stack = jnp.concatenate(
            [
                gl.astype(BF16),
                (gl * out[:hidden] * (1.0 - s0)).astype(BF16),
                gr.astype(BF16),
                (gr * out[2 * hidden : 3 * hidden] * (1.0 - s1)).astype(BF16),
            ],
            axis=0,
        )
        scaled = jnp.dot(back, stack, preferred_element_type=F32) * gain
        mean, centered, inverse = normalized(pair_ref, i)
        for part in range(A):
            at = pl.ds(pl.multiple_of((part * rows + i) * share, 8), share)
            left[at, :] = scaled[part * share : (part + 1) * share]
        one = jnp.sum(scaled, axis=0, keepdims=True)
        two = jnp.sum(scaled * centered, axis=0, keepdims=True) * inverse
        stat_buf[i] = jnp.concatenate([one, two, mean, inverse, one, one, one, one], axis=0)
        return carry

    for b in range(4):
        lax.fori_loop(b * n, (b + 1) * n, finish_row, 0, unroll=8)
        for copy in send_end(b):
            copy.start()

    for b in range(4):
        for copy in send_end(b):
            copy.wait()

        def combine(i, carry):
            kept_at = pl.ds(pl.multiple_of((a * rows + i) * share, 8), share)
            in_at = pl.ds(pl.multiple_of(i * share, 8), share)
            whole = left[kept_at, :] + scaled_in[in_at, :]
            stats = stat_buf[i]
            other = stat_in[i]
            one = (stats[0:1] + other[0:1]) * (1.0 / width)
            two = (stats[1:2] + other[1:2]) * (1.0 / width)
            inverse = stats[3:4]
            values = pair_ref[i, pl.ds(pl.multiple_of(a * share, 16), share), :].astype(F32)
            standard = (values - stats[2:3]) * inverse
            out_ref[i] = (whole - one - standard * two) * inverse
            return carry

        lax.fori_loop(b * n, (b + 1) * n, combine, 0, unroll=8)

    for d in range(1, R):
        piece(d).wait_send()
    for d in range(1, X):
        beside(d).wait_send()
        for s in range(R):
            swap(d, s, x).wait_send()
    for c in range(CHUNKS):
        if T > 1 or c < CHUNKS // 2:
            ring(0, c, True).wait_send()
        if T > 1 or c >= CHUNKS // 2:
            ring(0, c, False).wait_send()

    def drain(u, carry):
        t = u // CHUNKS
        c = u % CHUNKS
        cb = bwd_chunk(t, c)

        @pl.when(more(t, c, True))
        def _():
            ring(t + 1, c, True).wait_send()

        @pl.when(more(t, cb, False))
        def _():
            ring(t + 1, cb, False).wait_send()

        passed(t, c, True, a).wait_send()
        passed(t, cb, False, a).wait_send()
        return carry

    lax.fori_loop(0, units, drain, 0)


def local(dims, pair, grad_x, ln_gain, ln_bias, weights, chain_id, kept):
    R, X, A = dims
    rows, width, cols = pair.shape
    hidden = grad_x.shape[1]
    total = R * rows
    pack = cols // rows
    groups = hidden // (pack * X)
    pitch = total + 8
    gpitch = hidden + 8
    vmem = pl.BlockSpec(memory_space=pltpu.VMEM)
    proj = jnp.transpose(weights, (0, 2, 1)).reshape(4 * hidden, width)
    T = R // 2
    dma = pltpu.SemaphoreType.DMA
    return pl.pallas_call(
        functools.partial(main_kernel, dims),
        out_shape=jax.ShapeDtypeStruct((rows, width // A, cols), F32),
        in_specs=[vmem] * 7,
        out_specs=vmem,
        scratch_shapes=[
            pltpu.VMEM((R, rows, width, cols), BF16),
            pltpu.VMEM((hidden * pitch, cols), F32),
            pltpu.VMEM((hidden * pitch, cols), F32),
            pltpu.VMEM((max(X - 1, 1), rows, hidden, cols), BF16),
            pltpu.VMEM((X, rows * gpitch, cols), F32),
            pltpu.VMEM((R, groups, rows, cols), BF16),
            pltpu.VMEM((X, R, groups, rows, cols), BF16),
            pltpu.VMEM((total, cols), F32),
            pltpu.VMEM((hidden * rows, cols), F32),
            pltpu.VMEM((hidden * rows, cols), F32),
            pltpu.VMEM((rows, 8, cols), F32),
            pltpu.VMEM((rows * (width // A), cols), F32),
            pltpu.VMEM((rows, 8, cols), F32),
            dma((T, CHUNKS)),
            dma((T, CHUNKS)),
            dma((T, CHUNKS)),
            dma((T, CHUNKS)),
            dma((2, T, CHUNKS)),
            dma((2, T, CHUNKS)),
            dma((X,)),
            dma((X,)),
            dma((R,)),
            dma((R,)),
            dma((X, R)),
            dma((X, R)),
            dma((2, 4)),
            dma((2, 4)),
        ],
        compiler_params=pltpu.CompilerParams(
            collective_id=0, has_side_effects=True, vmem_limit_bytes=67043328
        ),
    )(pair, grad_x, ln_gain[None, :], ln_bias[None, :], proj, chain_id[None, :], kept)


def solution(mesh):
    placed = (
        P(("groups", "row"), None, "col"),
        P(("groups", "row"), "chan", "col"),
        P(),
        P(),
        P(None, None, "chan"),
        P("groups"),
        P("groups", None),
    )
    dims = (mesh.shape["row"], mesh.shape["col"], mesh.shape["chan"])
    return jax.shard_map(
        functools.partial(local, dims),
        mesh=mesh,
        in_specs=placed,
        out_specs=P(("groups", "row"), "chan", "col"),
        check_vma=False,
    )
```

profile of v0, /device:TPU:0, one launch (start us, length us, event | category | flops | bytes accessed | tf_op | source)
XLA Modules:
  0.0 71.9 jit_solution(17663687029336943736)
XLA Ops:
  0.0 69.6 %shard_map.73 = f32[32,64,128]{2,1,0:T(8,128)} custom-call(bf16[32,128,128]{2,1,0:T(8,128)(2,1)} %pair_ref.1, bf16[32,64,128]{2,1,0:T(8,128)(2,1)} %grad_ref.1, f32[1,128]{1,0:T(1,128)} %bitcast.8, f32[1,128]{1,0:T(1,128)} %bitcast.9, bf16[256,128]{1,0:T(8,128)(2,1)} %bitcast.6, s32[1,256]{1,0:T(1,128)} %bitcast.7, s32[16,16]{1,0:T(8,128)} %kept_ref.1), custom_call_target="tpu_custom_call" | custom-call | tf_op jit(solution)/shard_map/pallas_call | solution.py:458
  69.6 2.3 %copy.9 = f32[32,64,128]{2,1,0:T(8,128)} copy(f32[32,64,128]{2,1,0:T(8,128)} %shard_map.73) | data formatting | bytes 2097152
where the time goes:
time: 72.1 us; the launch traced here: 71.9 us
  Pallas kernels  69.6 us (97%)
  local copies, waits for them, and re-layouts  2.31 us (3%)
    pallas_call x1, Pallas kernels, local(): pl.pallas_call(functools.partial(main_kernel, dims), out_shape=jax.ShapeD...  69.6 us
    unnamed x1, local copies, waits for them, and re-layouts  2.31 us

commit v1 on v0

--- a/solution.py
+++ b/solution.py
@@ -1,4 +1,5 @@
 import functools
+import math
 
 import jax
 import jax.numpy as jnp
@@ -11,6 +12,7 @@
 F32 = jnp.float32
 BF16 = jnp.bfloat16
 CHUNKS = 4
+SPARE = 4 << 20
 
 
 def normalized(pair_ref, i):
@@ -23,6 +25,14 @@
 
 def main_kernel(
     dims,
+    pair_hbm,
+    grad_hbm,
+    gain_hbm,
+    bias_hbm,
+    proj_hbm,
+    chain_hbm,
+    kept_hbm,
+    out_ref,
     pair_ref,
     grad_ref,
     gain_ref,
@@ -30,7 +40,6 @@
     proj_ref,
     chain_ref,
     kept_ref,
-    out_ref,
     full,
     left,
     right,
@@ -44,10 +53,11 @@
     stat_buf,
     scaled_in,
     stat_in,
-    fwd_send,
-    fwd_recv,
-    bwd_send,
-    bwd_recv,
+    load_sem,
+    token,
+    ring_send,
+    ring_recv,
+    cross_send,
     pass_send,
     pass_recv,
     x_send,
@@ -90,9 +100,35 @@
     barrier = pltpu.get_barrier_semaphore()
     peers = [(g, r, x, sib)]
     peers += [(g, r, (x + d) % X, a) for d in range(1, X)]
-    peers += [(g, (r + d) % R, x, a) for d in range(1, R)]
+    peers += [(g, nxt, x, a)]
+    if R > 2:
+        peers += [(g, prv, x, a)]
+    mirror = R - 1 - p
+    to_mirror = (g, row_of(mirror), x, a)
+    if T > 2:
+        peers += [to_mirror]
     for peer in peers:
         pl.semaphore_signal(barrier, inc=1, device_id=peer, device_id_type=MESH)
+
+    def load(n, src, dst):
+        return pltpu.make_async_copy(src, dst, load_sem.at[n])
+
+    own = pl.ds(a * half, half)
+    other = pl.ds(sib * half, half)
+    loads = [
+        load(0, gain_hbm, gain_ref),
+        load(1, bias_hbm, bias_ref),
+        load(2, pair_hbm.at[own], pair_ref.at[own]),
+        load(3, pair_hbm.at[other], pair_ref.at[other]),
+        load(4, grad_hbm, grad_ref),
+        load(5, proj_hbm, proj_ref),
+        load(6, chain_hbm, chain_ref),
+        load(7, kept_hbm, kept_ref),
+    ]
+    for one in loads:
+        one.start()
+    for one in loads[:3]:
+        one.wait()
 
     gain = jnp.broadcast_to(gain_ref[...], (cols, width)).T
     bias = jnp.broadcast_to(bias_ref[...], (cols, width)).T
@@ -112,8 +148,8 @@
         return pltpu.make_async_remote_copy(
             src_ref=at,
             dst_ref=at,
-            send_sem=(fwd_send if forward else bwd_send).at[t, c],
-            recv_sem=(fwd_recv if forward else bwd_recv).at[t, c],
+            send_sem=ring_send.at[0 if forward else 1, t, c],
+            recv_sem=ring_recv.at[0 if forward else 1, t, c],
             device_id=(g, nxt if forward else prv, x, a),
             device_id_type=MESH,
         )
@@ -121,7 +157,30 @@
     def got(t, c, forward):
         block = row_of(p - 1 - t) if forward else row_of(p + 1 + t)
         at = full.at[block, pl.ds(a * half + c * step_rows, step_rows)]
-        return pltpu.make_async_copy(at, at, (fwd_recv if forward else bwd_recv).at[t, c])
+        return pltpu.make_async_copy(at, at, ring_recv.at[0 if forward else 1, t, c])
+
+    def corner(q):
+        q = (q + R) % R
+        return jnp.logical_or(
+            jnp.logical_or(q == 0, q == R - 1), jnp.logical_or(q == T - 1, q == T)
+        )
+
+    apart = (mirror + T - p + R) % R
+    across = jnp.logical_not(corner(p))
+    cross_forward = jnp.logical_and(across, apart > T)
+    cross_backward = jnp.logical_and(across, apart < T)
+    cross_step = jnp.where(apart > T, R - apart, apart) - 1
+
+    def cross(c):
+        at = full.at[row_of(mirror + T), pl.ds(a * half + c * step_rows, step_rows)]
+        return pltpu.make_async_remote_copy(
+            src_ref=at,
+            dst_ref=at,
+            send_sem=cross_send.at[c],
+            recv_sem=ring_recv.at[c // (CHUNKS // 2), last, c],
+            device_id=to_mirror,
+            device_id_type=MESH,
+        )
 
     def passed(t, c, forward, core):
         block = row_of(p - 1 - t) if forward else row_of(p + 1 + t)
@@ -138,7 +197,7 @@
 
     def beside(d):
         return pltpu.make_async_remote_copy(
-            src_ref=grad_ref,
+            src_ref=grad_hbm,
             dst_ref=grad_in.at[d - 1],
             send_sem=x_send.at[d - 1],
             recv_sem=x_recv.at[d - 1],
@@ -154,6 +213,23 @@
     for d in range(1, X):
         beside(d).start()
 
+    def signal_token(k):
+        pl.semaphore_signal(token.at[0, k], inc=1, device_id=(g, nxt, x, a), device_id_type=MESH)
+        pl.semaphore_signal(token.at[1, k], inc=1, device_id=(g, prv, x, a), device_id_type=MESH)
+
+    def relay(k):
+        pl.semaphore_wait(token.at[0, k], 1)
+        pl.semaphore_wait(token.at[1, k], 1)
+
+        @pl.when(k + 1 < last)
+        def _():
+            signal_token(k + 1)
+
+    if last > 0:
+        signal_token(0)
+
+    for one in loads[3:]:
+        one.wait()
     lax.fori_loop(0, half, functools.partial(normalize, sib), 0, unroll=4)
 
     chains = kept_ref.shape[0]
@@ -215,6 +291,7 @@
 
     def more(t, c, forward):
         split = c < CHUNKS // 2 if forward else c >= CHUNKS // 2
+        split = jnp.logical_and(split, corner(p + 1 if forward else p - 1))
         return jnp.logical_or(t + 1 < last, jnp.logical_and(t + 1 == last, split))
 
     def ring_step(u, carry):
@@ -227,6 +304,10 @@
         def _():
             ring(t + 1, c, True).start()
 
+        @pl.when(jnp.logical_and(cross_forward, t == cross_step))
+        def _():
+            cross(c).start()
+
         passed(t, c, True, a).start()
         got(t, cb, False).wait()
 
@@ -234,7 +315,15 @@
         def _():
             ring(t + 1, cb, False).start()
 
+        @pl.when(jnp.logical_and(cross_backward, t == cross_step))
+        def _():
+            cross(cb).start()
+
         passed(t, cb, False, a).start()
+
+        @pl.when(u < last)
+        def _():
+            relay(u)
 
         @pl.when(u > 0)
         def _():
@@ -264,7 +353,7 @@
             device_id_type=MESH,
         )
 
-    first = min(CHUNKS, units)
+    first = min(max(CHUNKS, last), units)
     lax.fori_loop(0, first, ring_step, 0)
 
     for d in range(1, X):
@@ -422,6 +511,11 @@
         if T > 1 or c >= CHUNKS // 2:
             ring(0, c, False).wait_send()
 
+    @pl.when(across)
+    def _():
+        for c in range(CHUNKS):
+            cross(c).wait_send()
+
     def drain(u, carry):
         t = u // CHUNKS
         c = u % CHUNKS
@@ -452,32 +546,38 @@
     pitch = total + 8
     gpitch = hidden + 8
     vmem = pl.BlockSpec(memory_space=pltpu.VMEM)
+    hbm = pl.BlockSpec(memory_space=pltpu.HBM)
     proj = jnp.transpose(weights, (0, 2, 1)).reshape(4 * hidden, width)
     T = R // 2
     dma = pltpu.SemaphoreType.DMA
+    args = (pair, grad_x, ln_gain[None, :], ln_bias[None, :], proj, chain_id[None, :], kept)
+    buffers = [pltpu.VMEM(arg.shape, arg.dtype) for arg in args] + [
+        pltpu.VMEM((R, rows, width, cols), BF16),
+        pltpu.VMEM((hidden * pitch, cols), F32),
+        pltpu.VMEM((hidden * pitch, cols), F32),
+        pltpu.VMEM((max(X - 1, 1), rows, hidden, cols), BF16),
+        pltpu.VMEM((X, rows * gpitch, cols), F32),
+        pltpu.VMEM((R, groups, rows, cols), BF16),
+        pltpu.VMEM((X, R, groups, rows, cols), BF16),
+        pltpu.VMEM((total, cols), F32),
+        pltpu.VMEM((hidden * rows, cols), F32),
+        pltpu.VMEM((hidden * rows, cols), F32),
+        pltpu.VMEM((rows, 8, cols), F32),
+        pltpu.VMEM((rows * (width // A), cols), F32),
+        pltpu.VMEM((rows, 8, cols), F32),
+    ]
+    need = sum(math.prod(one.shape) * jnp.dtype(one.dtype).itemsize for one in buffers)
     return pl.pallas_call(
         functools.partial(main_kernel, dims),
         out_shape=jax.ShapeDtypeStruct((rows, width // A, cols), F32),
-        in_specs=[vmem] * 7,
+        in_specs=[hbm] * 7,
         out_specs=vmem,
-        scratch_shapes=[
-            pltpu.VMEM((R, rows, width, cols), BF16),
-            pltpu.VMEM((hidden * pitch, cols), F32),
-            pltpu.VMEM((hidden * pitch, cols), F32),
-            pltpu.VMEM((max(X - 1, 1), rows, hidden, cols), BF16),
-            pltpu.VMEM((X, rows * gpitch, cols), F32),
-            pltpu.VMEM((R, groups, rows, cols), BF16),
-            pltpu.VMEM((X, R, groups, rows, cols), BF16),
-            pltpu.VMEM((total, cols), F32),
-            pltpu.VMEM((hidden * rows, cols), F32),
-            pltpu.VMEM((hidden * rows, cols), F32),
-            pltpu.VMEM((rows, 8, cols), F32),
-            pltpu.VMEM((rows * (width // A), cols), F32),
-            pltpu.VMEM((rows, 8, cols), F32),
-            dma((T, CHUNKS)),
-            dma((T, CHUNKS)),
-            dma((T, CHUNKS)),
-            dma((T, CHUNKS)),
+        scratch_shapes=buffers + [
+            dma((8,)),
+            pltpu.SemaphoreType.REGULAR((2, T)),
+            dma((2, T, CHUNKS)),
+            dma((2, T, CHUNKS)),
+            dma((CHUNKS,)),
             dma((2, T, CHUNKS)),
             dma((2, T, CHUNKS)),
             dma((X,)),
@@ -490,9 +590,9 @@
             dma((2, 4)),
         ],
         compiler_params=pltpu.CompilerParams(
-            collective_id=0, has_side_effects=True, vmem_limit_bytes=67043328
+            collective_id=0, has_side_effects=True, vmem_limit_bytes=min(67043328, need + SPARE)
         ),
-    )(pair, grad_x, ln_gain[None, :], ln_bias[None, :], proj, chain_id[None, :], kept)
+    )(*args)
 
 
 def solution(mesh):

time: 72.1 us -> 72.3 us (level)
  local copies, waits for them, and re-layouts: 2.31 us -> 5.47 us
  Pallas kernels: 69.6 us -> 66.5 us
    unnamed x1 -> x15, local copies, waits for them, and re-layouts: 2.31 us -> 5.47 us
    pallas_call x1, Pallas kernels: 69.6 us -> 66.5 us  [local(): pl.pallas_call(functools.partial(main_kernel, dims), out_shape=jax.ShapeD...]
where the time goes in v1:
time: 72.3 us; the launch traced here: 72 us
  Pallas kernels  66.5 us (92%)
  local copies, waits for them, and re-layouts  5.47 us (8%)
    pallas_call x1, Pallas kernels, local(): pl.pallas_call(functools.partial(main_kernel, dims), out_shape=jax.ShapeD...  66.5 us
    unnamed x15, local copies, waits for them, and re-layouts  5.47 us

profile of v1, /device:TPU:0, one launch (start us, length us, event | category | flops | bytes accessed | tf_op | source)
XLA Modules:
  0.0 72.0 jit_solution(9782989799514470953)
XLA Ops:
  0.0 0.0 copy-start.6
  0.0 0.0 copy-start.4
  0.0 0.0 copy-start.5
  0.0 0.6 copy-done.6
  0.7 0.0 copy-done.4
  0.7 0.0 copy-done.5
  0.7 0.0 copy-start
  0.7 1.2 %copy-done = bf16[32,128,128]{2,1,0:T(8,128)(2,1)S(1)} copy-done((bf16[32,128,128]{2,1,0:T(8,128)(2,1)S(1)}, bf16[32,128,128]{2,1,0:T(8,128)(2,1)}, u32[]{:S(2)}) %copy-start) | copy-done | bytes 1048600
  1.9 0.0 copy-start.1
  1.9 1.0 %copy-done.1 = bf16[32,64,128]{2,1,0:T(8,128)(2,1)S(1)} copy-done((bf16[32,64,128]{2,1,0:T(8,128)(2,1)S(1)}, bf16[32,64,128]{2,1,0:T(8,128)(2,1)}, u32[]{:S(2)}) %copy-start.1) | copy-done | bytes 524312
  3.0 0.0 copy-start.2
  3.0 0.8 %copy-done.2 = bf16[4,128,64]{1,2,0:T(8,128)(2,1)S(1)} copy-done((bf16[4,128,64]{1,2,0:T(8,128)(2,1)S(1)}, bf16[4,128,64]{1,2,0:T(8,128)(2,1)}, u32[]{:S(2)}) %copy-start.2) | copy-done | bytes 65560
  3.8 0.0 copy-start.3
  3.8 0.7 copy-done.3
  4.5 66.5 %shard_map.73 = f32[32,64,128]{2,1,0:T(8,128)S(1)} custom-call(bf16[32,128,128]{2,1,0:T(8,128)(2,1)S(1)} %copy-done, bf16[32,64,128]{2,1,0:T(8,128)(2,1)S(1)} %copy-done.1, f32[1,128]{1,0:T(1,128)S(1)} %bitcast.8, f32[1,128]{1,0:T(1,128)S(1)} %bitcast.9, bf16[256,128]{1,0:T(8,128)(2,1)S(1)} %bitcast.6, s32[1,256]{1,0:T(1,128)S(1)} %bitcast.7, ...), custom_call_target="tpu_custom_call" | custom-call | tf_op jit(solution)/shard_map/pallas_call | solution.py:570
  71.0 1.0 %copy.9 = f32[32,64,128]{2,1,0:T(8,128)} copy(f32[32,64,128]{2,1,0:T(8,128)S(1)} %shard_map.73) | data formatting | bytes 2097152
Async XLA Ops:
  0.0 0.7 copy-start.6
  0.0 0.7 copy-start.4
  0.0 0.7 copy-start.5
  0.7 1.2 %copy-start = (bf16[32,128,128]{2,1,0:T(8,128)(2,1)S(1)}, bf16[32,128,128]{2,1,0:T(8,128)(2,1)}, u32[]{:S(2)}) copy-start(bf16[32,128,128]{2,1,0:T(8,128)(2,1)} %pair_hbm.1) | copy-start | bytes 3145732
  1.9 1.0 %copy-start.1 = (bf16[32,64,128]{2,1,0:T(8,128)(2,1)S(1)}, bf16[32,64,128]{2,1,0:T(8,128)(2,1)}, u32[]{:S(2)}) copy-start(bf16[32,64,128]{2,1,0:T(8,128)(2,1)} %grad_hbm.1) | copy-start | bytes 1572868
  3.0 0.8 %copy-start.2 = (bf16[4,128,64]{1,2,0:T(8,128)(2,1)S(1)}, bf16[4,128,64]{1,2,0:T(8,128)(2,1)}, u32[]{:S(2)}) copy-start(bf16[4,128,64]{1,2,0:T(8,128)(2,1)} %param.11) | copy-start | bytes 196612
  3.8 0.7 copy-start.3

commit v2 on v1

--- a/solution.py
+++ b/solution.py
@@ -592,7 +592,7 @@
         compiler_params=pltpu.CompilerParams(
             collective_id=0, has_side_effects=True, vmem_limit_bytes=min(67043328, need + SPARE)
         ),
-    )(*args)
+    )(*[pltpu.with_memory_space_constraint(arg, pltpu.HBM) for arg in args])
 
 
 def solution(mesh):

time: 72.3 us -> 67.7 us (0.936)
  local copies, waits for them, and re-layouts: 5.47 us -> 0.97 us
    unnamed x15 -> x1, local copies, waits for them, and re-layouts: 5.47 us -> 0.97 us
where the time goes in v2:
time: 67.7 us; the launch traced here: 67.5 us
  Pallas kernels  66.5 us (98%)
  local copies, waits for them, and re-layouts  0.97 us (1%)
    pallas_call x1, Pallas kernels, local(): pl.pallas_call(functools.partial(main_kernel, dims), out_shape=jax.ShapeD...  66.5 us

profile of v2, /device:TPU:0, one launch (start us, length us, event | category | flops | bytes accessed | tf_op | source)
XLA Modules:
  0.0 67.5 jit_solution(15924889012833180632)
XLA Ops:
  0.0 66.5 %shard_map.73 = f32[32,64,128]{2,1,0:T(8,128)S(1)} custom-call(bf16[32,128,128]{2,1,0:T(8,128)(2,1)} %pair_hbm.1, bf16[32,64,128]{2,1,0:T(8,128)(2,1)} %grad_hbm.1, f32[1,128]{1,0:T(1,128)} %bitcast.8, f32[1,128]{1,0:T(1,128)} %bitcast.9, bf16[256,128]{1,0:T(8,128)(2,1)} %bitcast.6, s32[1,256]{1,0:T(1,128)} %bitcast.7, s32[16,16]{1,0:T(8,128)} %kept_hbm.1), custom_call_target="tpu_custom_call" | custom-call | tf_op jit(solution)/shard_map/pallas_call | solution.py:570
  66.6 1.0 %copy.9 = f32[32,64,128]{2,1,0:T(8,128)} copy(f32[32,64,128]{2,1,0:T(8,128)S(1)} %shard_map.73) | data formatting | bytes 2097152
